TPU v7x, 32 devices: a whole 2x2x4 slice. The times are simulated.
32 devices in a mesh: parts: 2 (over x), row: 8 (over z, core), col: 2 (over y).
Axes of the slice: x: 2, y: 2, z: 4, core: 2. Of those that a mesh axis runs over, the one named last changes fastest.
Arguments:
- pair_features_map: bfloat16 [64, 1024, 512], P(None, ('parts', 'row'), 'col'), parts along dimension 1, may hold values from -6 to 6
- labels: int32 [1024, 512], P(('parts', 'row', 'col')), parts along dimension 0, may hold values from 0 to 36, as said below
- lengths: int32 [2], P('parts'), parts along dimension 0, may hold values from 256 to 512
- conv_weight: bfloat16 [3, 3, 64, 64], replicated, may hold values from -0.25 to 0.25
- conv_bias: float32 [64], replicated, may hold values from -3 to 3
- head_weight: bfloat16 [37, 64], replicated, may hold values from -2.390625 to 2.390625
- head_bias: float32 [37], replicated, may hold values from -4 to 4
Outputs:
- pair_gradient: bfloat16 [64, 1024, 512], P(None, ('parts', 'row'), 'col'), parts along dimension 1
- grad_conv_weight: float32 [6, 3, 64, 64], P('parts'), parts along dimension 0
- grad_conv_bias: float32 [128], P('parts'), parts along dimension 0
- grad_head_weight: float32 [74, 64], P('parts'), parts along dimension 0
- grad_head_bias: float32 [74], P('parts'), parts along dimension 0
- loss: float32 [2], P('parts'), parts along dimension 0
There are 2 independent parts, one for each index of `parts`. A program takes and returns all parts, laid end to end along the dimension named above; an argument that names none is the same for every part. Nothing has to cross between parts.
Inputs may be any that keep to these rules, and one draw needn't show every extreme that they name: labels[i, j] equals labels[j, i] for every pair.
All inputs are finite; a program needn't handle non-finite values.
Results may differ from a plain program's by a relative error of at most 0.0067.
Values may be sent and summed in bfloat16 or wider, within the bound.
No kernel may reach another device: no remote copies, remote signals or barrier semaphores. Data moves between devices by JAX's collectives and lax.ppermute only.
A program may use at most 128 MiB of HBM per device.

v0:
```python
import jax
import jax.numpy as jnp
from jax import lax
from jax.sharding import PartitionSpec as P

DILATION_STEP = 4


def with_halo(cells, sides, width):
    for axis, dim in sides:
        count = lax.axis_size(axis)
        ends = count - 1
        head = lax.slice_in_dim(cells, 0, width, axis=dim)
        tail = lax.slice_in_dim(cells, cells.shape[dim] - width, cells.shape[dim], axis=dim)
        cells = jnp.concatenate(
            [
                lax.ppermute(tail, axis, [(i, (i + 1) % count) for i in range(ends)]),
                cells,
                lax.ppermute(head, axis, [((i + 1) % count, i) for i in range(ends)]),
            ],
            axis=dim,
        )
    return cells


def tile_to_band(field):
    channels, patch_rows, patch_columns = field.shape
    width = lax.axis_size("col")
    split = field.reshape(channels, width, patch_rows // width, patch_columns)
    moved = lax.all_to_all(split, "col", split_axis=1, concat_axis=3, tiled=True)
    return moved.reshape(channels, patch_rows // width, width * patch_columns)


def band_to_tile(field):
    channels, band_rows, length_cols = field.shape
    width = lax.axis_size("col")
    split = field.reshape(channels, band_rows, width, length_cols // width)
    moved = lax.all_to_all(split, "col", split_axis=2, concat_axis=1, tiled=True)
    return moved.reshape(channels, width * band_rows, length_cols // width)


def reorder_back(moved, channels, band_rows, length_cols):
    return jnp.transpose(moved, (0, 3, 2, 1)).reshape(channels, band_rows, length_cols)


def mirror_features(field):
    channels, band_rows, length_cols = field.shape
    bands = lax.axis_size(("row", "col"))
    blocks = field.reshape(channels, band_rows, bands, band_rows)
    moved = lax.all_to_all(blocks, ("row", "col"), split_axis=2, concat_axis=2, tiled=True)
    return reorder_back(moved, channels, band_rows, length_cols)


def per_device(pair_features_map, labels, lengths, conv_weight, conv_bias, head_weight, head_bias):
    channels, patch_rows, patch_columns = pair_features_map.shape
    nbins = head_weight.shape[0]
    bordered_input = with_halo(pair_features_map, (("row", 1), ("col", 2)), DILATION_STEP)
    before_activation = (
        jnp.zeros((channels, patch_rows, patch_columns), jnp.float32) + conv_bias[:, None, None]
    )
    for offset_row in range(3):
        for offset_column in range(3):
            sliding_patch = bordered_input[
                :,
                DILATION_STEP * offset_row : DILATION_STEP * offset_row + patch_rows,
                DILATION_STEP * offset_column : DILATION_STEP * offset_column + patch_columns,
            ]
            before_activation = before_activation + jnp.einsum(
                "oc,cij->oij",
                conv_weight[offset_row, offset_column],
                sliding_patch,
                preferred_element_type=jnp.float32,
            )
    hidden_tile = jnp.where(
        before_activation > 0, before_activation, jnp.expm1(jnp.minimum(before_activation, 0.0))
    ).astype(jnp.bfloat16)
    hidden = tile_to_band(hidden_tile)
    band_rows, length_cols = (hidden.shape[1], hidden.shape[2])
    hidden_mirror = mirror_features(hidden)
    direct = jnp.einsum("kc,cij->kij", head_weight, hidden, preferred_element_type=jnp.float32)
    opposite = jnp.einsum(
        "kc,cij->kij", head_weight, hidden_mirror, preferred_element_type=jnp.float32
    )
    logits = 0.5 * (direct + opposite) + head_bias[:, None, None]
    band = lax.axis_index(("row", "col"))
    row_ids = band * band_rows + lax.broadcasted_iota(jnp.int32, (band_rows, length_cols), 0)
    col_ids = lax.broadcasted_iota(jnp.int32, (band_rows, length_cols), 1)
    extent = lengths[0]
    valid = ((row_ids < extent) & (col_ids < extent)).astype(jnp.float32)
    count = (extent * extent).astype(jnp.float32)
    onehot = (lax.broadcasted_iota(jnp.int32, (nbins, 1, 1), 0) == labels[None]).astype(jnp.float32)
    lse = jnp.log(jnp.sum(jnp.exp(logits), axis=0))
    picked = jnp.sum(onehot * logits, axis=0)
    loss_local = jnp.sum(valid * (lse - picked))
    dlogits = (valid[None] * (jnp.exp(logits - lse[None]) - onehot) / count).astype(jnp.bfloat16)
    head_grad = jnp.einsum("kij,cij->kc", dlogits, hidden, preferred_element_type=jnp.float32)
    head_bias_grad = jnp.sum(dlogits.astype(jnp.float32), axis=(1, 2))
    tile_grad = band_to_tile(dlogits)
    back = jnp.einsum("kc,kij->cij", head_weight, tile_grad, preferred_element_type=jnp.float32)
    slope = jnp.where(before_activation > 0, 1.0, jnp.exp(jnp.minimum(before_activation, 0.0)))
    preact_gradient = (back * slope).astype(jnp.bfloat16)
    preact_gradient_bordered = with_halo(preact_gradient, (("row", 1), ("col", 2)), DILATION_STEP)
    grad_field = jnp.zeros((channels, patch_rows, patch_columns), jnp.float32)
    tap_rows = []
    for offset_row in range(3):
        tap_cols = []
        for offset_column in range(3):
            sliding_patch = bordered_input[
                :,
                DILATION_STEP * offset_row : DILATION_STEP * offset_row + patch_rows,
                DILATION_STEP * offset_column : DILATION_STEP * offset_column + patch_columns,
            ]
            tap_cols.append(
                jnp.einsum(
                    "oij,cij->oc",
                    preact_gradient,
                    sliding_patch,
                    preferred_element_type=jnp.float32,
                )
            )
            row_begin = DILATION_STEP * (2 - offset_row)
            column_begin = DILATION_STEP * (2 - offset_column)
            source = preact_gradient_bordered[
                :, row_begin : row_begin + patch_rows, column_begin : column_begin + patch_columns
            ]
            grad_field = grad_field + jnp.einsum(
                "oc,oij->cij",
                conv_weight[offset_row, offset_column],
                source,
                preferred_element_type=jnp.float32,
            )
        tap_rows.append(jnp.stack(tap_cols))
    conv_grad = jnp.stack(tap_rows)
    conv_bias_grad = jnp.sum(preact_gradient.astype(jnp.float32), axis=(1, 2))
    conv_grad, conv_bias_grad, head_grad, head_bias_grad, loss_total = lax.psum(
        (conv_grad, conv_bias_grad, head_grad, head_bias_grad, loss_local), ("row", "col")
    )
    loss = (loss_total / count).reshape(1)
    return (
        grad_field.astype(jnp.bfloat16),
        conv_grad,
        conv_bias_grad,
        head_grad,
        head_bias_grad,
        loss,
    )


def solution(mesh):
    return jax.shard_map(
        per_device,
        mesh=mesh,
        in_specs=(
            P(None, ("parts", "row"), "col"),
            P(("parts", "row", "col"), None),
            P("parts"),
            P(),
            P(),
            P(),
            P(),
        ),
        out_specs=(
            P(None, ("parts", "row"), "col"),
            P("parts", None, None, None),
            P("parts"),
            P("parts", None),
            P("parts"),
            P("parts"),
        ),
        check_vma=False,
    )
```

profile of v0, /device:TPU:0, one launch (start us, length us, event | category | flops | bytes accessed | tf_op | source)
XLA Modules:
  0.0 410.8 jit_solution(8611053157606536604)
XLA Ops:
  13.8 4.4 %fusion.60 = f32[64,64,256]{2,0,1:T(8,128)} fusion(bf16[3,3,64,64]{3,2,1,0:T(8,128)(2,1)} %param.10, bf16[64,64,256]{2,1,0:T(8,128)(2,1)S(1)} %copy-done.10), kind=kOutput, calls=%fused_computation.100 | convolution fusion | flops 134217728 | bytes 6307840 | tf_op jit(solution)/shard_map/oc,cij->oij/dot_general | solution.py:68
  25.1 4.9 %collective-permute-start.2 = (bf16[64,72,4]{1,0,2:T(8,128)(2,1)}, bf16[64,72,4]{1,0,2:T(8,128)(2,1)}, u32[]{:S(2)}, u32[]{:S(2)}) collective-permute-start(bf16[64,72,4]{1,0,2:T(8,128)(2,1)} %copy.58), channel_id=1, source_target_pairs={{0,1},{2,3},{4,5},{6,7},{8,9},{10,11},{12,13},{14,15},{16,17},{18,... | collective-permute-start | bytes 110600 | tf_op jit(solution)/shard_map/ppermute | solution.py:17
  33.7 4.3 %fusion.41 = f32[64,256,64]{1,2,0:T(8,128)} fusion(bf16[64,64,256]{2,0,1:T(8,128)(2,1)} %copy-done.7, bf16[64,4,256]{2,0,1:T(8,128)(2,1)} %copy-done.23, bf16[3,3,64,64]{3,2,1,0:T(8,128)(2,1)} %param.10), kind=kOutput, calls=%fused_computation.67 | convolution fusion | flops 138412032 | bytes 6438912 | tf_op jit(solution)/shard_map/oc,cij->oij/dot_general | solution.py:68
  44.2 3.6 fusion.63
  47.8 3.6 fusion.71
  54.3 3.8 fusion.66
  58.1 3.9 fusion.56
  62.1 3.8 fusion.47
  65.9 13.3 %fusion = (bf16[64,64,256]{2,0,1:T(8,128)(2,1)S(1)}, f32[64,64,256]{2,0,1:T(8,128)}) fusion(bf16[64,72,4]{2,0,1:T(8,128)(2,1)S(1)} %copy.62, bf16[64,72,256]{2,0,1:T(8,128)(2,1)S(1)} %constant_dynamic-update-slice_fusion, bf16[3,3,64,64]{3,2,1,0:T(8,128)(2,1)} %param.10, f32[64,256,64]{1,2,0:T(8,128)} %fusion.43, f32[64,256,64]{1,2,0:T(8,128)} %fusion.47, ...), kind=kOutput, calls=%fused_computation.6 | convolution fusion | flops 152043520 | bytes 42258688 | tf_op jit(solution)/shard_map/oc,cij->oij/dot_general | solution.py:68
  80.4 29.7 %all_to_all.35 = bf16[64,2,32,256]{3,2,0,1:T(8,128)(2,1)} all-to-all(bf16[64,2,32,256]{3,2,0,1:T(8,128)(2,1)S(1)} %copy.65), channel_id=1, replica_groups=mesh['parts'=2,'row'=8,'col'=2] {'col'}, dimensions={1} | all-to-all | bytes 4194304 | tf_op jit(solution)/shard_map/all_to_all | solution.py:30
  110.1 5.0 %copy.66 = bf16[64,2,32,256]{0,3,1,2:T(8,128)(2,1)} copy(bf16[64,2,32,256]{3,2,0,1:T(8,128)(2,1)} %all_to_all.35) | data formatting | bytes 4194304 | tf_op jit(solution)/shard_map/all_to_all | solution.py:30
  115.0 5.3 %copy.126 = bf16[64,32,16,32]{0,3,1,2:T(8,128)(2,1)} copy(bf16[64,32,16,32]{0,3,2,1:T(8,128)(2,1)} %bitcast.202) | data formatting | bytes 4194304 | tf_op jit(solution)/shard_map/reshape;reshape | solution.py:49
  120.3 7.5 %reshape.99 = bf16[16,2,32768]{2,1,0:T(2,128)(2,1)} reshape(bf16[16,32,32,64]{3,2,1,0:T(8,128)(2,1)} %bitcast.205) | data formatting | bytes 4194304
  127.9 6.9 %all-to-all-start.1 = ((bf16[16,2,32768]{2,1,0:T(2,128)(2,1)}), bf16[16,2,32768]{2,1,0:T(2,128)(2,1)}, u32[]{:S(2)}, u32[]{:S(2)}) async-start(bf16[16,2,32768]{2,1,0:T(2,128)(2,1)} %reshape.99), calls=%async_computation.1 | async-start | bytes 4194304 | tf_op jit(solution)/shard_map/all_to_all | solution.py:50
  136.7 6.1 %fusion.93 = f32[32,512,37]{1,2,0:T(8,128)} fusion(bf16[64,32,512]{0,2,1:T(8,128)(2,1)} %bitcast.203, bf16[37,64]{1,0:T(8,128)(2,1)S(1)} %copy-done), kind=kOutput, calls=%fused_computation.133 | convolution fusion | flops 77594624 | bytes 4526720 | tf_op jit(solution)/shard_map/kc,cij->kij/dot_general | solution.py:80
  142.9 34.0 %all-to-all-done.1 = bf16[16,2,32768]{2,1,0:T(2,128)(2,1)} async-done(((bf16[16,2,32768]{2,1,0:T(2,128)(2,1)}), bf16[16,2,32768]{2,1,0:T(2,128)(2,1)}, u32[]{:S(2)}, u32[]{:S(2)}) %all-to-all-start.1) | async-done | bytes 2097184 | tf_op jit(solution)/shard_map/all_to_all | solution.py:50
  176.9 7.4 %reshape.100 = bf16[16,32,32,64]{3,2,1,0:T(8,128)(2,1)} reshape(bf16[16,2,32768]{2,1,0:T(2,128)(2,1)} %all-to-all-done.1) | data formatting | bytes 4194304
  184.3 7.9 %fusion.10 = (f32[32,512]{1,0:T(8,128)S(1)}, f32[32,512]{1,0:T(8,128)S(1)}, f32[32,512,37]{1,2,0:T(8,128)S(1)}) fusion(s32[32,512]{1,0:T(8,128)} %param.8, f32[37]{0:T(128)} %param.13, f32[32,512,37]{1,2,0:T(8,128)} %fusion.93, bf16[37,64]{1,0:T(8,128)(2,1)S(1)} %copy-done, bf16[64,32,512]{0,1,2:T(8,128)(2,1)} %bitcast.207), kind=kOutput, calls=%fused_computation.32 | convolution fusion | flops 81805312 | bytes 7148308 | tf_op jit(solution)/shard_map/kc,cij->kij/dot_general | solution.py:81
  195.1 3.8 reshape.98
  201.5 4.5 %all-to-all-start.2 = ((bf16[37,32,2,256]{3,1,0,2:T(8,128)(2,1)}), bf16[37,32,2,256]{3,1,0,2:T(8,128)(2,1)}, u32[]{:S(2)}, u32[]{:S(2)}) async-start(bf16[37,32,2,256]{3,1,0,2:T(8,128)(2,1)} %copy.72), calls=%async_computation.2 | async-start | bytes 2424832 | tf_op jit(solution)/shard_map/all_to_all | solution.py:38
  206.2 4.1 convolution_bitcast_fusion.7
  210.3 10.8 %all-to-all-done.2 = bf16[37,32,2,256]{3,1,0,2:T(8,128)(2,1)} async-done(((bf16[37,32,2,256]{3,1,0,2:T(8,128)(2,1)}), bf16[37,32,2,256]{3,1,0,2:T(8,128)(2,1)}, u32[]{:S(2)}, u32[]{:S(2)}) %all-to-all-start.2) | async-done | bytes 1212448 | tf_op jit(solution)/shard_map/all_to_all | solution.py:38
  223.1 4.2 %convert_reduce_fusion = (f32[64]{0:T(128)}, bf16[64,64,256]{2,0,1:T(8,128)(2,1)S(1)}) fusion(f32[64,64,256]{2,0,1:T(8,128)} %get-tuple-element.45, bf16[37,64,256]{2,0,1:T(8,128)(2,1)S(1)} %bitcast.208, bf16[37,64]{1,0:T(8,128)(2,1)S(1)} %copy-done), kind=kOutput, calls=%fused_computation.17 | convolution fusion | flops 84934592 | bytes 7508864 | tf_op jit(solution)/shard_map/kc,kij->cij/dot_general | solution.py:99
  238.1 3.6 fusion.58
  243.0 4.4 %collective-permute-start.4 = (bf16[64,4,256]{2,0,1:T(8,128)(2,1)S(1)}, bf16[64,4,256]{2,0,1:T(8,128)(2,1)S(1)}, u32[]{:S(2)}, u32[]{:S(2)}) collective-permute-start(bf16[64,4,256]{2,0,1:T(8,128)(2,1)S(1)} %get-tuple-element.39), channel_id=1, source_target_pairs={{0,2},{2,4},{4,6},{6,8},{8,10},{10,12},{12,14},{1,3},{3,5},{5,7},{... | collective-permute-start | bytes 393224 | tf_op jit(solution)/shard_map/ppermute | solution.py:17
  249.0 62.7 %all-reduce = (f32[64]{0:T(128)}, f32[37,64]{1,0:T(8,128)}, f32[37]{0:T(128)}, f32[]{:T(128)}) all-reduce(f32[64]{0:T(128)S(1)} %copy-done.30, f32[37,64]{1,0:T(8,128)S(1)} %copy-done.26, f32[37]{0:T(128)S(1)} %get-tuple-element.30, f32[]{:T(128)} %get-tuple-element.42), channel_id=1, replica_groups=mesh['parts'=2,'row'=8,'col'=2] {'row','col'}, use_global_device_ids=true, to_apply=%region_3.4 | all-reduce | flops 2470 | bytes 19760 | tf_op jit(solution)/shard_map/psum | solution.py:135
  324.1 5.9 %collective-permute-start.7 = (bf16[64,72,4]{1,0,2:T(8,128)(2,1)}, bf16[64,72,4]{1,0,2:T(8,128)(2,1)}, u32[]{:S(2)}, u32[]{:S(2)}) collective-permute-start(bf16[64,72,4]{1,0,2:T(8,128)(2,1)} %copy.78), channel_id=1, source_target_pairs={{0,1},{2,3},{4,5},{6,7},{8,9},{10,11},{12,13},{14,15},{16,17},{18,... | collective-permute-start | bytes 110600 | tf_op jit(solution)/shard_map/ppermute | solution.py:17
  330.0 3.5 fusion.12
  339.8 3.7 copy.79
  343.5 6.5 %maximum_maximum_fusion = (bf16[64,72,260]{2,0,1:T(8,128)(2,1)S(1)}, bf16[64,72,260]{2,0,1:T(8,128)(2,1)S(1)}) fusion(bf16[64,4,256]{2,0,1:T(8,128)(2,1)S(1)} %copy-done.16, bf16[64,64,256]{2,0,1:T(8,128)(2,1)S(1)} %copy-done.3, bf16[64,4,256]{2,0,1:T(8,128)(2,1)S(1)} %copy-done.18, bf16[64,72,4]{2,0,1:T(8,128)(2,1)} %copy.79, bf16[64,72,4]{2,0,1:T(8,128)(2,1)S(1)} %copy.75), kind=kLoop, calls=%fused_computation.23 | loop fusion | flops 19169280 | bytes 7225344 | tf_op jit(solution)/shard_map/concatenate | solution.py:15
  364.3 10.8 %fusion.24 = bf16[64,64,256]{2,0,1:T(8,128)(2,1)S(1)} fusion(f32[64,256,64]{1,2,0:T(8,128)} %fusion.16, f32[64,256,64]{1,2,0:T(8,128)} %fusion.29, f32[64,256,64]{1,2,0:T(8,128)} %fusion.31, f32[64,256,64]{1,2,0:T(8,128)S(1)} %copy-done.12, f32[64,256,64]{1,2,0:T(8,128)} %fusion.33, f32[64,256,64]{1,2,0:T(8,128)} %fusion.35, f32[64,256,64]{1,2,0:T(8,128)} %fusion.37, ...), kind=kOutput, calls=%fused_computation.50 | convolution fusion | flops 143654912 | bytes 37765120 | tf_op jit(solution)/shard_map/oc,oij->cij/dot_general | solution.py:126
  377.5 23.2 %all-reduce.3.cloned.1.call-done = f32[3,3,64,64]{3,2,1,0:T(8,128)} async-done(((f32[3,3,64,64]{3,2,1,0:T(8,128)}), f32[3,3,64,64]{3,2,1,0:T(8,128)}) %all-reduce.3.cloned.1.call-update) | async-done | bytes 147472 | tf_op jit(solution)/shard_map/psum | solution.py:135
  (124 shorter events, 86.2 us)
Async XLA Ops:
  7.2 129.6 %copy-start = (bf16[37,64]{1,0:T(8,128)(2,1)S(1)}, bf16[37,64]{1,0:T(8,128)(2,1)}, u32[]{:S(2)}) copy-start(bf16[37,64]{1,0:T(8,128)(2,1)} %param.12) | copy-start | bytes 14212
  7.2 6.6 %copy-start.10 = (bf16[64,64,256]{2,1,0:T(8,128)(2,1)S(1)}, bf16[64,64,256]{2,1,0:T(8,128)(2,1)}, u32[]{:S(2)}) copy-start(bf16[64,64,256]{2,1,0:T(8,128)(2,1)} %param.7) | copy-start | bytes 6291460
  10.1 8.1 %copy-start.7 = (bf16[64,64,256]{2,0,1:T(8,128)(2,1)}, bf16[64,64,256]{2,0,1:T(8,128)(2,1)S(1)}, u32[]{:S(2)}) copy-start(bf16[64,64,256]{2,0,1:T(8,128)(2,1)S(1)} %copy.55) | copy-start | bytes 6291460
  10.2 8.1 %collective-permute-start = (bf16[64,4,256]{2,0,1:T(8,128)(2,1)S(1)}, bf16[64,4,256]{2,0,1:T(8,128)(2,1)S(1)}, u32[]{:S(2)}, u32[]{:S(2)}) collective-permute-start(bf16[64,4,256]{2,0,1:T(8,128)(2,1)S(1)} %get-tuple-element.40), channel_id=1, source_target_pairs={{0,2},{2,4},{4,6},{6,8},{8,10},{10,12},{12,14},{1,3},{3,5},{5,7},{... | collective-permute-start | bytes 393224 | tf_op jit(solution)/shard_map/ppermute | solution.py:17
  12.5 6.9 %collective-permute-start.1 = (bf16[64,4,256]{2,0,1:T(8,128)(2,1)S(1)}, bf16[64,4,256]{2,0,1:T(8,128)(2,1)S(1)}, u32[]{:S(2)}, u32[]{:S(2)}) collective-permute-start(bf16[64,4,256]{2,0,1:T(8,128)(2,1)S(1)} %get-tuple-element.41), channel_id=1, source_target_pairs={{2,0},{4,2},{6,4},{8,6},{10,8},{12,10},{14,12},{3,1},{5,3},{7,5},{... | collective-permute-start | bytes 393224 | tf_op jit(solution)/shard_map/ppermute | solution.py:19
  25.1 16.2 %collective-permute-start.2 = (bf16[64,72,4]{1,0,2:T(8,128)(2,1)}, bf16[64,72,4]{1,0,2:T(8,128)(2,1)}, u32[]{:S(2)}, u32[]{:S(2)}) collective-permute-start(bf16[64,72,4]{1,0,2:T(8,128)(2,1)} %copy.58), channel_id=1, source_target_pairs={{0,1},{2,3},{4,5},{6,7},{8,9},{10,11},{12,13},{14,15},{16,17},{18,... | collective-permute-start | bytes 110600 | tf_op jit(solution)/shard_map/ppermute | solution.py:17
  32.0 5.9 %copy-start.8 = (bf16[64,64,256]{2,0,1:T(8,128)(2,1)S(1)}, bf16[64,64,256]{2,0,1:T(8,128)(2,1)}, u32[]{:S(2)}) copy-start(bf16[64,64,256]{2,0,1:T(8,128)(2,1)} %copy-done.7) | copy-start | bytes 6291460
  32.0 5.9 %copy-start.21 = (bf16[64,4,256]{2,0,1:T(8,128)(2,1)S(1)}, bf16[64,4,256]{2,0,1:T(8,128)(2,1)}, u32[]{:S(2)}) copy-start(bf16[64,4,256]{2,0,1:T(8,128)(2,1)} %copy-done.20) | copy-start | bytes 393220
  32.0 19.4 %collective-permute-start.3 = (bf16[64,72,4]{1,0,2:T(8,128)(2,1)}, bf16[64,72,4]{1,0,2:T(8,128)(2,1)}, u32[]{:S(2)}, u32[]{:S(2)}) collective-permute-start(bf16[64,72,4]{1,0,2:T(8,128)(2,1)} %copy.61), channel_id=1, source_target_pairs={{1,0},{3,2},{5,4},{7,6},{9,8},{11,10},{13,12},{15,14},{17,16},{19,... | collective-permute-start | bytes 110600 | tf_op jit(solution)/shard_map/ppermute | solution.py:19
  58.1 3.9 copy-start.5
  62.1 3.8 copy-start.13
  62.1 3.8 copy-start.31
  127.9 49.0 %all-to-all-start.1 = ((bf16[16,2,32768]{2,1,0:T(2,128)(2,1)}), bf16[16,2,32768]{2,1,0:T(2,128)(2,1)}, u32[]{:S(2)}, u32[]{:S(2)}) async-start(bf16[16,2,32768]{2,1,0:T(2,128)(2,1)} %reshape.99), calls=%async_computation.1 | async-start | bytes 4194304 | tf_op jit(solution)/shard_map/all_to_all | solution.py:50
  184.3 7.9 %copy-start.29 = (pred[32]{0:T(512)(128)(4,1)S(1)}, pred[32]{0:T(512)(128)(4,1)}, u32[]{:S(2)}) copy-start(pred[32]{0:T(512)(128)(4,1)} %copy-done.28) | copy-start | bytes 100
  184.3 8.6 %copy-start.25 = (f32[32,512]{1,0:T(8,128)S(1)}, f32[32,512]{1,0:T(8,128)}, u32[]{:S(2)}) copy-start(f32[32,512]{1,0:T(8,128)} %and_convert_fusion) | copy-start | bytes 196612
  184.3 8.6 %copy-start.27 = (s32[32,512]{1,0:T(8,128)S(1)}, s32[32,512]{1,0:T(8,128)}, u32[]{:S(2)}) copy-start(s32[32,512]{1,0:T(8,128)} %param.8) | copy-start | bytes 196612
  201.5 19.6 %all-to-all-start.2 = ((bf16[37,32,2,256]{3,1,0,2:T(8,128)(2,1)}), bf16[37,32,2,256]{3,1,0,2:T(8,128)(2,1)}, u32[]{:S(2)}, u32[]{:S(2)}) async-start(bf16[37,32,2,256]{3,1,0,2:T(8,128)(2,1)} %copy.72), calls=%async_computation.2 | async-start | bytes 2424832 | tf_op jit(solution)/shard_map/all_to_all | solution.py:38
  206.0 194.7 %all-reduce.3.cloned.1.call-start = ((), (), s32[]{:S(2)}) async-start(), calls=%async_computation.3 | async-start | bytes 589824 | tf_op jit(solution)/shard_map/psum | solution.py:135
  227.3 20.9 %copy-start.2 = (bf16[64,64,256]{2,0,1:T(8,128)(2,1)}, bf16[64,64,256]{2,0,1:T(8,128)(2,1)S(1)}, u32[]{:S(2)}) copy-start(bf16[64,64,256]{2,0,1:T(8,128)(2,1)S(1)} %get-tuple-element.48) | copy-start | bytes 6291460
  238.1 9.4 %copy-start.9 = (bf16[64,64,256]{2,0,1:T(8,128)(2,1)S(1)}, bf16[64,64,256]{2,0,1:T(8,128)(2,1)}, u32[]{:S(2)}) copy-start(bf16[64,64,256]{2,0,1:T(8,128)(2,1)} %copy-done.7) | copy-start | bytes 6291460
  238.1 9.4 %copy-start.24 = (bf16[64,4,256]{2,0,1:T(8,128)(2,1)S(1)}, bf16[64,4,256]{2,0,1:T(8,128)(2,1)}, u32[]{:S(2)}) copy-start(bf16[64,4,256]{2,0,1:T(8,128)(2,1)} %copy-done.23) | copy-start | bytes 393220
  241.7 71.4 %collective-permute-start.5 = (bf16[64,4,256]{2,0,1:T(8,128)(2,1)S(1)}, bf16[64,4,256]{2,0,1:T(8,128)(2,1)S(1)}, u32[]{:S(2)}, u32[]{:S(2)}) collective-permute-start(bf16[64,4,256]{2,0,1:T(8,128)(2,1)S(1)} %get-tuple-element.38), channel_id=1, source_target_pairs={{2,0},{4,2},{6,4},{8,6},{10,8},{12,10},{14,12},{3,1},{5,3},{7,5},{... | collective-permute-start | bytes 393224 | tf_op jit(solution)/shard_map/ppermute | solution.py:19
  243.0 5.2 %copy-start.22 = (bf16[64,4,256]{2,0,1:T(8,128)(2,1)S(1)}, bf16[64,4,256]{2,0,1:T(8,128)(2,1)}, u32[]{:S(2)}) copy-start(bf16[64,4,256]{2,0,1:T(8,128)(2,1)} %copy-done.20) | copy-start | bytes 393220
  243.0 70.1 %collective-permute-start.4 = (bf16[64,4,256]{2,0,1:T(8,128)(2,1)S(1)}, bf16[64,4,256]{2,0,1:T(8,128)(2,1)S(1)}, u32[]{:S(2)}, u32[]{:S(2)}) collective-permute-start(bf16[64,4,256]{2,0,1:T(8,128)(2,1)S(1)} %get-tuple-element.39), channel_id=1, source_target_pairs={{0,2},{2,4},{4,6},{6,8},{8,10},{10,12},{12,14},{1,3},{3,5},{5,7},{... | collective-permute-start | bytes 393224 | tf_op jit(solution)/shard_map/ppermute | solution.py:17
  318.0 12.0 %copy-start.3 = (bf16[64,64,256]{2,0,1:T(8,128)(2,1)S(1)}, bf16[64,64,256]{2,0,1:T(8,128)(2,1)}, u32[]{:S(2)}) copy-start(bf16[64,64,256]{2,0,1:T(8,128)(2,1)} %copy-done.2) | copy-start | bytes 6291460
  318.0 12.0 %copy-start.15 = (bf16[64,4,256]{2,0,1:T(8,128)(2,1)S(1)}, bf16[64,4,256]{2,0,1:T(8,128)(2,1)}, u32[]{:S(2)}) copy-start(bf16[64,4,256]{2,0,1:T(8,128)(2,1)} %copy-done.14) | copy-start | bytes 393220
  320.8 16.2 %collective-permute-start.6 = (bf16[64,72,4]{1,0,2:T(8,128)(2,1)S(1)}, bf16[64,72,4]{1,0,2:T(8,128)(2,1)}, u32[]{:S(2)}, u32[]{:S(2)}) collective-permute-start(bf16[64,72,4]{1,0,2:T(8,128)(2,1)S(1)} %copy.74), channel_id=1, source_target_pairs={{1,0},{3,2},{5,4},{7,6},{9,8},{11,10},{13,12},{15,14},{17,16},{19,... | collective-permute-start | bytes 110600 | tf_op jit(solution)/shard_map/ppermute | solution.py:19
  324.1 9.4 %copy-start.18 = (bf16[64,4,256]{2,0,1:T(8,128)(2,1)S(1)}, bf16[64,4,256]{2,0,1:T(8,128)(2,1)}, u32[]{:S(2)}) copy-start(bf16[64,4,256]{2,0,1:T(8,128)(2,1)} %copy-done.17) | copy-start | bytes 393220
  324.1 15.7 %collective-permute-start.7 = (bf16[64,72,4]{1,0,2:T(8,128)(2,1)}, bf16[64,72,4]{1,0,2:T(8,128)(2,1)}, u32[]{:S(2)}, u32[]{:S(2)}) collective-permute-start(bf16[64,72,4]{1,0,2:T(8,128)(2,1)} %copy.78), channel_id=1, source_target_pairs={{0,1},{2,3},{4,5},{6,7},{8,9},{10,11},{12,13},{14,15},{16,17},{18,... | collective-permute-start | bytes 110600 | tf_op jit(solution)/shard_map/ppermute | solution.py:17
  337.0 6.6 %copy-start.16 = (bf16[64,4,256]{2,0,1:T(8,128)(2,1)S(1)}, bf16[64,4,256]{2,0,1:T(8,128)(2,1)}, u32[]{:S(2)}) copy-start(bf16[64,4,256]{2,0,1:T(8,128)(2,1)} %copy-done.14) | copy-start | bytes 393220
  343.5 6.5 %copy-start.19 = (bf16[3,3,64,64]{3,2,1,0:T(8,128)(2,1)S(1)}, bf16[3,3,64,64]{3,2,1,0:T(8,128)(2,1)}, u32[]{:S(2)}) copy-start(bf16[3,3,64,64]{3,2,1,0:T(8,128)(2,1)} %param.10) | copy-start | bytes 221188
  364.3 38.2 %copy-start.1 = (bf16[37,64]{1,0:T(8,128)(2,1)S(1)}, bf16[37,64]{1,0:T(8,128)(2,1)}, u32[]{:S(2)}) copy-start(bf16[37,64]{1,0:T(8,128)(2,1)} %param.12) | copy-start | bytes 14212
  (11 other events, 15.4 us)
Sparse Core Ops, SparseCore 0:
  313.2 87.4 all-reduce.2
where the time goes:
time: 418 us; the launch traced here: 411 us
  matrix products  113 us (27%)
  blocking collectives  92.3 us (22%)
  local copies, waits for them, and re-layouts  72.9 us (17%)
  waiting for transfers between devices  68.1 us (16%)
  starting transfers between devices  34.7 us (8%)
  between operations  17.4 us (4%)
  other arithmetic  12.7 us (3%)
    psum x1, blocking collectives, per_device(): lax.psum((conv_grad, conv_bias_grad, head_grad, head_bias_grad, loss_loca...  62.7 us
    dot_general x9, matrix products, per_device(): jnp.einsum('oc,cij->oij', conv_weight[offset_row, offset_column], sliding...  44.2 us
    dot_general x9, matrix products, per_device(): jnp.einsum('oc,oij->cij', conv_weight[offset_row, offset_column], source,...  35.5 us
    all_to_all x1, waiting for transfers between devices, mirror_features(): lax.all_to_all(blocks, ('row', 'col'), split_axis=2, concat_axis=2, tiled...  34 us
    all_to_all x1, blocking collectives, tile_to_band(): lax.all_to_all(split, 'col', split_axis=1, concat_axis=3, tiled=True)  29.7 us
    unnamed x71, local copies, waits for them, and re-layouts  27.2 us
    psum x1, waiting for transfers between devices, per_device(): lax.psum((conv_grad, conv_bias_grad, head_grad, head_bias_grad, loss_loca...  23.2 us
    ppermute x4, starting transfers between devices, with_halo(): lax.ppermute(tail, axis, [(i, (i + 1) % count) for i in range(ends)])  17.6 us
  transfers between devices with their start and end apart: 11, of which 3 were waited for; matrix products, arithmetic and copies ran while one was open for 23% of the time, Pallas kernels for 0%

commit v1 on v0

--- a/solution.py
+++ b/solution.py
@@ -4,6 +4,29 @@
 from jax.sharding import PartitionSpec as P
 
 DILATION_STEP = 4
+
+
+def split_up(x, dim, size):
+    before, after = (x.shape[:dim], x.shape[dim + 1 :])
+    return jnp.moveaxis(x.reshape(*before, size, -1, *after), dim, 0)
+
+
+def joined_along(parts, dim):
+    parts = jnp.moveaxis(parts, 0, dim)
+    lengths = parts.shape
+    return parts.reshape(*lengths[:dim], lengths[dim] * lengths[dim + 1], *lengths[dim + 2 :])
+
+
+def sent_to_each(x, axis, split_dim, concat_dim):
+    count, here = (lax.axis_size(axis), lax.axis_index(axis))
+    blocks = split_up(x, split_dim, count)
+    out = blocks
+    for step in range(1, count):
+        target, source = ((here + step) % count, (here - step) % count)
+        sent = lax.dynamic_index_in_dim(blocks, target, 0)
+        other = lax.ppermute(sent, axis, [(i, (i + step) % count) for i in range(count)])
+        out = lax.dynamic_update_slice_in_dim(out, other, source, axis=0)
+    return joined_along(out, concat_dim)
 
 
 def with_halo(cells, sides, width):
@@ -47,7 +70,7 @@
     channels, band_rows, length_cols = field.shape
     bands = lax.axis_size(("row", "col"))
     blocks = field.reshape(channels, band_rows, bands, band_rows)
-    moved = lax.all_to_all(blocks, ("row", "col"), split_axis=2, concat_axis=2, tiled=True)
+    moved = sent_to_each(blocks, ("row", "col"), 2, 2)
     return reorder_back(moved, channels, band_rows, length_cols)
 
 

time: 418 us -> 448 us (1.072)
  starting transfers between devices: 34.7 us -> 95.7 us
  blocking collectives: 92.3 us -> 60 us
  waiting for transfers between devices: 68.1 us -> 88.9 us
  local copies, waits for them, and re-layouts: 72.9 us -> 60.5 us
  matrix products: 113 us -> 104 us
    ppermute x0 -> x15, starting transfers between devices: none -> 64.3 us  [sent_to_each(): lax.ppermute(sent, axis, [(i, (i + step) % count) for i in range(count)])]
    ppermute x0 -> x15, waiting for transfers between devices: none -> 35 us  [sent_to_each(): lax.ppermute(sent, axis, [(i, (i + step) % count) for i in range(count)])]
    all_to_all x1 -> x0, blocking collectives: 29.7 us -> none  [tile_to_band(): lax.all_to_all(split, 'col', split_axis=1, concat_axis=3, tiled=True)]
    unnamed x71 -> x64, local copies, waits for them, and re-layouts: 27.2 us -> 12.2 us
    all_to_all x1, waiting for transfers between devices: 34 us -> 23.7 us  [tile_to_band(): lax.all_to_all(split, 'col', split_axis=1, concat_axis=3, tiled=True)]
    another operation x1 -> x0, local copies, waits for them, and re-layouts: 5.31 us -> none  [mirror_features(): blocks = field.reshape(channels, band_rows, bands, band_rows)]
    dot_general x1, matrix products: 7.86 us -> 2.65 us  [per_device(): jnp.einsum('kc,cij->kij', head_weight, hidden_mirror, preferred_element_t...]
    all_to_all x1, waiting for transfers between devices: 10.8 us -> 6.06 us  [band_to_tile(): lax.all_to_all(split, 'col', split_axis=2, concat_axis=1, tiled=True)]
  transfers between devices with their start and end apart: 11 -> 26, of which waited for: 3 -> 7; matrix products, arithmetic and copies ran while one was open for 23% -> 21% of each run, Pallas kernels for 0% -> 0%
where the time goes in v1:
time: 448 us; the launch traced here: 440 us
  matrix products  104 us (23%)
  starting transfers between devices  95.7 us (21%)
  waiting for transfers between devices  88.9 us (20%)
  local copies, waits for them, and re-layouts  60.5 us (14%)
  blocking collectives  60 us (13%)
  between operations  18.3 us (4%)
  other arithmetic  12.7 us (3%)
    ppermute x15, starting transfers between devices, sent_to_each(): lax.ppermute(sent, axis, [(i, (i + step) % count) for i in range(count)])  64.3 us
    psum x1, blocking collectives, per_device(): lax.psum((conv_grad, conv_bias_grad, head_grad, head_bias_grad, loss_loca...  60 us
    dot_general x9, matrix products, per_device(): jnp.einsum('oc,cij->oij', conv_weight[offset_row, offset_column], sliding...  44.3 us
    dot_general x9, matrix products, per_device(): jnp.einsum('oc,oij->cij', conv_weight[offset_row, offset_column], source,...  35.6 us
    ppermute x15, waiting for transfers between devices, sent_to_each(): lax.ppermute(sent, axis, [(i, (i + step) % count) for i in range(count)])  35 us
    psum x1, waiting for transfers between devices, per_device(): lax.psum((conv_grad, conv_bias_grad, head_grad, head_bias_grad, loss_loca...  24.1 us
    all_to_all x1, waiting for transfers between devices, tile_to_band(): lax.all_to_all(split, 'col', split_axis=1, concat_axis=3, tiled=True)  23.7 us
    ppermute x4, starting transfers between devices, with_halo(): lax.ppermute(tail, axis, [(i, (i + 1) % count) for i in range(ends)])  16.4 us
  transfers between devices with their start and end apart: 26, of which 7 were waited for; matrix products, arithmetic and copies ran while one was open for 21% of the time, Pallas kernels for 0%

profile of v1, /device:TPU:0, one launch (start us, length us, event | category | flops | bytes accessed | tf_op | source)
XLA Modules:
  0.0 440.3 jit_solution(14428799395273393095)
XLA Ops:
  13.8 4.4 fusion.56
  25.1 4.9 %collective-permute-start.2 = (bf16[64,72,4]{1,0,2:T(8,128)(2,1)}, bf16[64,72,4]{1,0,2:T(8,128)(2,1)}, u32[]{:S(2)}, u32[]{:S(2)}) collective-permute-start(bf16[64,72,4]{1,0,2:T(8,128)(2,1)} %copy.58), channel_id=1, source_target_pairs={{0,1},{2,3},{4,5},{6,7},{8,9},{10,11},{12,13},{14,15},{16,17},{18,... | collective-permute-start | bytes 110600 | tf_op jit(solution)/shard_map/ppermute | solution.py:40
  33.6 4.3 fusion.37
  47.8 3.6 fusion.67
  54.3 3.8 fusion.62
  58.1 4.0 fusion.52
  62.2 3.8 fusion.43
  66.0 13.3 %fusion = (bf16[64,64,256]{2,0,1:T(8,128)(2,1)S(1)}, f32[64,64,256]{2,0,1:T(8,128)}) fusion(bf16[64,72,4]{2,0,1:T(8,128)(2,1)S(1)} %copy.62, bf16[64,72,256]{2,0,1:T(8,128)(2,1)S(1)} %constant_dynamic-update-slice_fusion, bf16[3,3,64,64]{3,2,1,0:T(8,128)(2,1)} %param.10, f32[64,256,64]{1,2,0:T(8,128)} %fusion.39, f32[64,256,64]{1,2,0:T(8,128)} %fusion.43, ...), kind=kOutput, calls=%fused_computation.6 | convolution fusion | flops 152043520 | bytes 42258688 | tf_op jit(solution)/shard_map/oc,cij->oij/dot_general | solution.py:91
  81.9 4.8 %all-to-all-start = ((bf16[64,2,32,256]{3,2,0,1:T(8,128)(2,1)}), bf16[64,2,32,256]{3,2,0,1:T(8,128)(2,1)}, u32[]{:S(2)}, u32[]{:S(2)}) async-start(bf16[64,2,32,256]{3,2,0,1:T(8,128)(2,1)} %copy.65), calls=%async_computation | async-start | bytes 4194304 | tf_op jit(solution)/shard_map/all_to_all | solution.py:53
  89.3 23.7 %all-to-all-done = bf16[64,2,32,256]{3,2,0,1:T(8,128)(2,1)} async-done(((bf16[64,2,32,256]{3,2,0,1:T(8,128)(2,1)}), bf16[64,2,32,256]{3,2,0,1:T(8,128)(2,1)}, u32[]{:S(2)}, u32[]{:S(2)}) %all-to-all-start) | async-done | bytes 2097184 | tf_op jit(solution)/shard_map/all_to_all | solution.py:53
  113.0 5.0 %copy.66 = bf16[64,2,32,256]{0,3,1,2:T(8,128)(2,1)} copy(bf16[64,2,32,256]{3,2,0,1:T(8,128)(2,1)} %all-to-all-done) | data formatting | bytes 4194304 | tf_op jit(solution)/shard_map/all_to_all | solution.py:53
  125.9 4.2 collective-permute-start.6
  136.5 3.9 collective-permute-start.11
  141.1 4.9 %collective-permute-start.12 = (bf16[1,64,32,1,32]{1,4,0,2,3:T(8,128)(2,1)S(1)}, bf16[1,64,32,1,32]{1,4,0,2,3:T(8,128)(2,1)S(1)}, u32[]{:S(2)}, u32[]{:S(2)}) collective-permute-start(bf16[1,64,32,1,32]{1,4,0,2,3:T(8,128)(2,1)S(1)} %get-tuple-element.38), channel_id=1, source_target_pairs={{0,9},{1,10},{2,11},{3,12},{4,13},{5,14},{6,15},{7,0},{8,1},{9,2},... | collective-permute-start | bytes 393224 | tf_op jit(solution)/shard_map/ppermute | solution.py:27
  146.0 28.4 %collective-permute-done.8 = bf16[1,64,32,1,32]{1,4,0,2,3:T(8,128)(2,1)S(1)} collective-permute-done((bf16[1,64,32,1,32]{1,4,0,2,3:T(8,128)(2,1)S(1)}, bf16[1,64,32,1,32]{1,4,0,2,3:T(8,128)(2,1)S(1)}, u32[]{:S(2)}, u32[]{:S(2)}) %collective-permute-start.8) | collective-permute-done | bytes 131104 | tf_op jit(solution)/shard_map/ppermute | solution.py:27
  176.7 13.6 %collective-permute-start.14 = (bf16[1,64,32,1,32]{1,4,0,2,3:T(8,128)(2,1)S(1)}, bf16[1,64,32,1,32]{1,4,0,2,3:T(8,128)(2,1)S(1)}, u32[]{:S(2)}, u32[]{:S(2)}) collective-permute-start(bf16[1,64,32,1,32]{1,4,0,2,3:T(8,128)(2,1)S(1)} %get-tuple-element.36), channel_id=1, source_target_pairs={{0,11},{1,12},{2,13},{3,14},{4,15},{5,0},{6,1},{7,2},{8,3},{9,4},{... | collective-permute-start | bytes 393224 | tf_op jit(solution)/shard_map/ppermute | solution.py:27
  190.4 12.7 %collective-permute-start.15 = (bf16[1,64,32,1,32]{1,4,0,2,3:T(8,128)(2,1)S(1)}, bf16[1,64,32,1,32]{1,4,0,2,3:T(8,128)(2,1)S(1)}, u32[]{:S(2)}, u32[]{:S(2)}) collective-permute-start(bf16[1,64,32,1,32]{1,4,0,2,3:T(8,128)(2,1)S(1)} %get-tuple-element.35), channel_id=1, source_target_pairs={{0,12},{1,13},{2,14},{3,15},{4,0},{5,1},{6,2},{7,3},{8,4},{9,5},{1... | collective-permute-start | bytes 393224 | tf_op jit(solution)/shard_map/ppermute | solution.py:27
  203.1 5.6 %collective-permute-start.16 = (bf16[1,64,32,1,32]{1,4,0,2,3:T(8,128)(2,1)S(1)}, bf16[1,64,32,1,32]{1,4,0,2,3:T(8,128)(2,1)S(1)}, u32[]{:S(2)}, u32[]{:S(2)}) collective-permute-start(bf16[1,64,32,1,32]{1,4,0,2,3:T(8,128)(2,1)S(1)} %get-tuple-element.34), channel_id=1, source_target_pairs={{0,13},{1,14},{2,15},{3,0},{4,1},{5,2},{6,3},{7,4},{8,5},{9,6},{10... | collective-permute-start | bytes 393224 | tf_op jit(solution)/shard_map/ppermute | solution.py:27
  208.7 6.1 %collective-permute-start.17 = (bf16[1,64,32,1,32]{1,4,0,2,3:T(8,128)(2,1)S(1)}, bf16[1,64,32,1,32]{1,4,0,2,3:T(8,128)(2,1)S(1)}, u32[]{:S(2)}, u32[]{:S(2)}) collective-permute-start(bf16[1,64,32,1,32]{1,4,0,2,3:T(8,128)(2,1)S(1)} %get-tuple-element.33), channel_id=1, source_target_pairs={{0,14},{1,15},{2,0},{3,1},{4,2},{5,3},{6,4},{7,5},{8,6},{9,7},{10,... | collective-permute-start | bytes 393224 | tf_op jit(solution)/shard_map/ppermute | solution.py:27
  214.8 6.0 %collective-permute-start.18 = (bf16[1,64,32,1,32]{1,4,0,2,3:T(8,128)(2,1)S(1)}, bf16[1,64,32,1,32]{1,4,0,2,3:T(8,128)(2,1)S(1)}, u32[]{:S(2)}, u32[]{:S(2)}) collective-permute-start(bf16[1,64,32,1,32]{1,4,0,2,3:T(8,128)(2,1)S(1)} %get-tuple-element.32), channel_id=1, source_target_pairs={{0,15},{1,0},{2,1},{3,2},{4,3},{5,4},{6,5},{7,6},{8,7},{9,8},{10,9... | collective-permute-start | bytes 393224 | tf_op jit(solution)/shard_map/ppermute | solution.py:27
  221.1 3.6 collective-permute-done.18
  233.1 3.8 reshape.117
  239.5 4.5 %all-to-all-start.1 = ((bf16[37,32,2,256]{3,1,0,2:T(8,128)(2,1)}), bf16[37,32,2,256]{3,1,0,2:T(8,128)(2,1)}, u32[]{:S(2)}, u32[]{:S(2)}) async-start(bf16[37,32,2,256]{3,1,0,2:T(8,128)(2,1)} %copy.71), calls=%async_computation.1 | async-start | bytes 2424832 | tf_op jit(solution)/shard_map/all_to_all | solution.py:61
  244.2 4.1 convolution_bitcast_fusion.7
  248.2 6.1 %all-to-all-done.1 = bf16[37,32,2,256]{3,1,0,2:T(8,128)(2,1)} async-done(((bf16[37,32,2,256]{3,1,0,2:T(8,128)(2,1)}), bf16[37,32,2,256]{3,1,0,2:T(8,128)(2,1)}, u32[]{:S(2)}, u32[]{:S(2)}) %all-to-all-start.1) | async-done | bytes 1212448 | tf_op jit(solution)/shard_map/all_to_all | solution.py:61
  256.3 4.2 convert_reduce_fusion
  281.1 60.0 %all-reduce = (f32[64]{0:T(128)}, f32[37,64]{1,0:T(8,128)}, f32[37]{0:T(128)}, f32[]{:T(128)}) all-reduce(f32[64]{0:T(128)S(1)} %copy-done.27, f32[37,64]{1,0:T(8,128)S(1)} %copy-done.23, f32[37]{0:T(128)S(1)} %get-tuple-element.30, f32[]{:T(128)} %get-tuple-element.57), channel_id=1, replica_groups=mesh['parts'=2,'row'=8,'col'=2] {'row','col'}, use_global_device_ids=true, to_apply=%region_3.4 | all-reduce | flops 2470 | bytes 19760 | tf_op jit(solution)/shard_map/psum | solution.py:158
  352.7 5.8 %collective-permute-start.22 = (bf16[64,72,4]{1,0,2:T(8,128)(2,1)}, bf16[64,72,4]{1,0,2:T(8,128)(2,1)}, u32[]{:S(2)}, u32[]{:S(2)}) collective-permute-start(bf16[64,72,4]{1,0,2:T(8,128)(2,1)} %copy.77), channel_id=1, source_target_pairs={{0,1},{2,3},{4,5},{6,7},{8,9},{10,11},{12,13},{14,15},{16,17},{18,... | collective-permute-start | bytes 110600 | tf_op jit(solution)/shard_map/ppermute | solution.py:40
  368.3 3.7 copy.78
  372.0 6.5 %maximum_maximum_fusion = (bf16[64,72,260]{2,0,1:T(8,128)(2,1)S(1)}, bf16[64,72,260]{2,0,1:T(8,128)(2,1)S(1)}) fusion(bf16[64,4,256]{2,0,1:T(8,128)(2,1)S(1)} %collective-permute-done.20, bf16[64,64,256]{2,0,1:T(8,128)(2,1)S(1)} %copy-done.3, bf16[64,4,256]{2,0,1:T(8,128)(2,1)S(1)} %collective-permute-done.19, bf16[64,72,4]{2,0,1:T(8,128)(2,1)} %copy.78, ...), kind=kLoop, calls=%fused_computation.21 | loop fusion | flops 19169280 | bytes 7225344 | tf_op jit(solution)/shard_map/concatenate | solution.py:38
  392.8 10.8 %fusion.22 = bf16[64,64,256]{2,0,1:T(8,128)(2,1)S(1)} fusion(f32[64,256,64]{1,2,0:T(8,128)} %fusion.14, f32[64,256,64]{1,2,0:T(8,128)} %fusion.27, f32[64,256,64]{1,2,0:T(8,128)} %fusion.29, f32[64,256,64]{1,2,0:T(8,128)S(1)} %copy-done.13, f32[64,256,64]{1,2,0:T(8,128)} %fusion.31, f32[64,256,64]{1,2,0:T(8,128)} %fusion.33, f32[64,256,64]{1,2,0:T(8,128)} %fusion.35, ...), kind=kOutput, calls=%fused_computation.48 | convolution fusion | flops 143654912 | bytes 37765120 | tf_op jit(solution)/shard_map/oc,oij->cij/dot_general | solution.py:149
  406.1 24.1 %all-reduce.3.cloned.1.call-done = f32[3,3,64,64]{3,2,1,0:T(8,128)} async-done(((f32[3,3,64,64]{3,2,1,0:T(8,128)}), f32[3,3,64,64]{3,2,1,0:T(8,128)}) %all-reduce.3.cloned.1.call-update) | async-done | bytes 147472 | tf_op jit(solution)/shard_map/psum | solution.py:158
  (162 shorter events, 124.1 us)
Async XLA Ops:
  7.2 115.0 %copy-start = (bf16[37,64]{1,0:T(8,128)(2,1)S(1)}, bf16[37,64]{1,0:T(8,128)(2,1)}, u32[]{:S(2)}) copy-start(bf16[37,64]{1,0:T(8,128)(2,1)} %param.12) | copy-start | bytes 14212
  10.2 8.1 %collective-permute-start = (bf16[64,4,256]{2,0,1:T(8,128)(2,1)S(1)}, bf16[64,4,256]{2,0,1:T(8,128)(2,1)S(1)}, u32[]{:S(2)}, u32[]{:S(2)}) collective-permute-start(bf16[64,4,256]{2,0,1:T(8,128)(2,1)S(1)} %get-tuple-element.55), channel_id=1, source_target_pairs={{0,2},{2,4},{4,6},{6,8},{8,10},{10,12},{12,14},{1,3},{3,5},{5,7},{... | collective-permute-start | bytes 393224 | tf_op jit(solution)/shard_map/ppermute | solution.py:40
  12.5 6.9 %collective-permute-start.1 = (bf16[64,4,256]{2,0,1:T(8,128)(2,1)S(1)}, bf16[64,4,256]{2,0,1:T(8,128)(2,1)S(1)}, u32[]{:S(2)}, u32[]{:S(2)}) collective-permute-start(bf16[64,4,256]{2,0,1:T(8,128)(2,1)S(1)} %get-tuple-element.56), channel_id=1, source_target_pairs={{2,0},{4,2},{6,4},{8,6},{10,8},{12,10},{14,12},{3,1},{5,3},{7,5},{... | collective-permute-start | bytes 393224 | tf_op jit(solution)/shard_map/ppermute | solution.py:42
  25.1 16.3 %collective-permute-start.2 = (bf16[64,72,4]{1,0,2:T(8,128)(2,1)}, bf16[64,72,4]{1,0,2:T(8,128)(2,1)}, u32[]{:S(2)}, u32[]{:S(2)}) collective-permute-start(bf16[64,72,4]{1,0,2:T(8,128)(2,1)} %copy.58), channel_id=1, source_target_pairs={{0,1},{2,3},{4,5},{6,7},{8,9},{10,11},{12,13},{14,15},{16,17},{18,... | collective-permute-start | bytes 110600 | tf_op jit(solution)/shard_map/ppermute | solution.py:40
  32.0 19.5 %collective-permute-start.3 = (bf16[64,72,4]{1,0,2:T(8,128)(2,1)}, bf16[64,72,4]{1,0,2:T(8,128)(2,1)}, u32[]{:S(2)}, u32[]{:S(2)}) collective-permute-start(bf16[64,72,4]{1,0,2:T(8,128)(2,1)} %copy.61), channel_id=1, source_target_pairs={{1,0},{3,2},{5,4},{7,6},{9,8},{11,10},{13,12},{15,14},{17,16},{19,... | collective-permute-start | bytes 110600 | tf_op jit(solution)/shard_map/ppermute | solution.py:42
  81.9 31.1 %all-to-all-start = ((bf16[64,2,32,256]{3,2,0,1:T(8,128)(2,1)}), bf16[64,2,32,256]{3,2,0,1:T(8,128)(2,1)}, u32[]{:S(2)}, u32[]{:S(2)}) async-start(bf16[64,2,32,256]{3,2,0,1:T(8,128)(2,1)} %copy.65), calls=%async_computation | async-start | bytes 4194304 | tf_op jit(solution)/shard_map/all_to_all | solution.py:53
  121.0 11.1 %collective-permute-start.4 = (bf16[1,64,32,1,32]{1,4,0,2,3:T(8,128)(2,1)S(1)}, bf16[1,64,32,1,32]{1,4,0,2,3:T(8,128)(2,1)S(1)}, u32[]{:S(2)}, u32[]{:S(2)}) collective-permute-start(bf16[1,64,32,1,32]{1,4,0,2,3:T(8,128)(2,1)S(1)} %get-tuple-element.46), channel_id=1, source_target_pairs={{0,1},{1,2},{2,3},{3,4},{4,5},{5,6},{6,7},{7,8},{8,9},{9,10},{10,1... | collective-permute-start | bytes 393224 | tf_op jit(solution)/shard_map/ppermute | solution.py:27
  121.1 12.7 %collective-permute-start.5 = (bf16[1,64,32,1,32]{1,4,0,2,3:T(8,128)(2,1)S(1)}, bf16[1,64,32,1,32]{1,4,0,2,3:T(8,128)(2,1)S(1)}, u32[]{:S(2)}, u32[]{:S(2)}) collective-permute-start(bf16[1,64,32,1,32]{1,4,0,2,3:T(8,128)(2,1)S(1)} %get-tuple-element.45), channel_id=1, source_target_pairs={{0,2},{1,3},{2,4},{3,5},{4,6},{5,7},{6,8},{7,9},{8,10},{9,11},{10,... | collective-permute-start | bytes 393224 | tf_op jit(solution)/shard_map/ppermute | solution.py:27
  125.9 10.6 %collective-permute-start.6 = (bf16[1,64,32,1,32]{1,4,0,2,3:T(8,128)(2,1)S(1)}, bf16[1,64,32,1,32]{1,4,0,2,3:T(8,128)(2,1)S(1)}, u32[]{:S(2)}, u32[]{:S(2)}) collective-permute-start(bf16[1,64,32,1,32]{1,4,0,2,3:T(8,128)(2,1)S(1)} %get-tuple-element.44), channel_id=1, source_target_pairs={{0,3},{1,4},{2,5},{3,6},{4,7},{5,8},{6,9},{7,10},{8,11},{9,12},{10... | collective-permute-start | bytes 393224 | tf_op jit(solution)/shard_map/ppermute | solution.py:27
  130.1 11.0 %collective-permute-start.7 = (bf16[1,64,32,1,32]{1,4,0,2,3:T(8,128)(2,1)S(1)}, bf16[1,64,32,1,32]{1,4,0,2,3:T(8,128)(2,1)S(1)}, u32[]{:S(2)}, u32[]{:S(2)}) collective-permute-start(bf16[1,64,32,1,32]{1,4,0,2,3:T(8,128)(2,1)S(1)} %get-tuple-element.43), channel_id=1, source_target_pairs={{0,4},{1,5},{2,6},{3,7},{4,8},{5,9},{6,10},{7,11},{8,12},{9,13},{1... | collective-permute-start | bytes 393224 | tf_op jit(solution)/shard_map/ppermute | solution.py:27
  131.6 42.7 %collective-permute-start.8 = (bf16[1,64,32,1,32]{1,4,0,2,3:T(8,128)(2,1)S(1)}, bf16[1,64,32,1,32]{1,4,0,2,3:T(8,128)(2,1)S(1)}, u32[]{:S(2)}, u32[]{:S(2)}) collective-permute-start(bf16[1,64,32,1,32]{1,4,0,2,3:T(8,128)(2,1)S(1)} %get-tuple-element.42), channel_id=1, source_target_pairs={{0,5},{1,6},{2,7},{3,8},{4,9},{5,10},{6,11},{7,12},{8,13},{9,14},{... | collective-permute-start | bytes 393224 | tf_op jit(solution)/shard_map/ppermute | solution.py:27
  132.1 44.6 %collective-permute-start.9 = (bf16[1,64,32,1,32]{1,4,0,2,3:T(8,128)(2,1)S(1)}, bf16[1,64,32,1,32]{1,4,0,2,3:T(8,128)(2,1)S(1)}, u32[]{:S(2)}, u32[]{:S(2)}) collective-permute-start(bf16[1,64,32,1,32]{1,4,0,2,3:T(8,128)(2,1)S(1)} %get-tuple-element.41), channel_id=1, source_target_pairs={{0,6},{1,7},{2,8},{3,9},{4,10},{5,11},{6,12},{7,13},{8,14},{9,15},... | collective-permute-start | bytes 393224 | tf_op jit(solution)/shard_map/ppermute | solution.py:27
  133.7 56.7 %collective-permute-start.10 = (bf16[1,64,32,1,32]{1,4,0,2,3:T(8,128)(2,1)S(1)}, bf16[1,64,32,1,32]{1,4,0,2,3:T(8,128)(2,1)S(1)}, u32[]{:S(2)}, u32[]{:S(2)}) collective-permute-start(bf16[1,64,32,1,32]{1,4,0,2,3:T(8,128)(2,1)S(1)} %get-tuple-element.40), channel_id=1, source_target_pairs={{0,7},{1,8},{2,9},{3,10},{4,11},{5,12},{6,13},{7,14},{8,15},{9,0},... | collective-permute-start | bytes 393224 | tf_op jit(solution)/shard_map/ppermute | solution.py:27
  136.5 66.6 %collective-permute-start.11 = (bf16[1,64,32,1,32]{1,4,0,2,3:T(8,128)(2,1)S(1)}, bf16[1,64,32,1,32]{1,4,0,2,3:T(8,128)(2,1)S(1)}, u32[]{:S(2)}, u32[]{:S(2)}) collective-permute-start(bf16[1,64,32,1,32]{1,4,0,2,3:T(8,128)(2,1)S(1)} %get-tuple-element.39), channel_id=1, source_target_pairs={{0,8},{1,9},{2,10},{3,11},{4,12},{5,13},{6,14},{7,15},{8,0},{9,1},... | collective-permute-start | bytes 393224 | tf_op jit(solution)/shard_map/ppermute | solution.py:27
  141.1 67.6 %collective-permute-start.12 = (bf16[1,64,32,1,32]{1,4,0,2,3:T(8,128)(2,1)S(1)}, bf16[1,64,32,1,32]{1,4,0,2,3:T(8,128)(2,1)S(1)}, u32[]{:S(2)}, u32[]{:S(2)}) collective-permute-start(bf16[1,64,32,1,32]{1,4,0,2,3:T(8,128)(2,1)S(1)} %get-tuple-element.38), channel_id=1, source_target_pairs={{0,9},{1,10},{2,11},{3,12},{4,13},{5,14},{6,15},{7,0},{8,1},{9,2},... | collective-permute-start | bytes 393224 | tf_op jit(solution)/shard_map/ppermute | solution.py:27
  174.4 40.4 %collective-permute-start.13 = (bf16[1,64,32,1,32]{1,4,0,2,3:T(8,128)(2,1)S(1)}, bf16[1,64,32,1,32]{1,4,0,2,3:T(8,128)(2,1)S(1)}, u32[]{:S(2)}, u32[]{:S(2)}) collective-permute-start(bf16[1,64,32,1,32]{1,4,0,2,3:T(8,128)(2,1)S(1)} %get-tuple-element.37), channel_id=1, source_target_pairs={{0,10},{1,11},{2,12},{3,13},{4,14},{5,15},{6,0},{7,1},{8,2},{9,3},... | collective-permute-start | bytes 393224 | tf_op jit(solution)/shard_map/ppermute | solution.py:27
  176.7 44.1 %collective-permute-start.14 = (bf16[1,64,32,1,32]{1,4,0,2,3:T(8,128)(2,1)S(1)}, bf16[1,64,32,1,32]{1,4,0,2,3:T(8,128)(2,1)S(1)}, u32[]{:S(2)}, u32[]{:S(2)}) collective-permute-start(bf16[1,64,32,1,32]{1,4,0,2,3:T(8,128)(2,1)S(1)} %get-tuple-element.36), channel_id=1, source_target_pairs={{0,11},{1,12},{2,13},{3,14},{4,15},{5,0},{6,1},{7,2},{8,3},{9,4},{... | collective-permute-start | bytes 393224 | tf_op jit(solution)/shard_map/ppermute | solution.py:27
  190.4 30.5 %collective-permute-start.15 = (bf16[1,64,32,1,32]{1,4,0,2,3:T(8,128)(2,1)S(1)}, bf16[1,64,32,1,32]{1,4,0,2,3:T(8,128)(2,1)S(1)}, u32[]{:S(2)}, u32[]{:S(2)}) collective-permute-start(bf16[1,64,32,1,32]{1,4,0,2,3:T(8,128)(2,1)S(1)} %get-tuple-element.35), channel_id=1, source_target_pairs={{0,12},{1,13},{2,14},{3,15},{4,0},{5,1},{6,2},{7,3},{8,4},{9,5},{1... | collective-permute-start | bytes 393224 | tf_op jit(solution)/shard_map/ppermute | solution.py:27
  203.1 17.9 %collective-permute-start.16 = (bf16[1,64,32,1,32]{1,4,0,2,3:T(8,128)(2,1)S(1)}, bf16[1,64,32,1,32]{1,4,0,2,3:T(8,128)(2,1)S(1)}, u32[]{:S(2)}, u32[]{:S(2)}) collective-permute-start(bf16[1,64,32,1,32]{1,4,0,2,3:T(8,128)(2,1)S(1)} %get-tuple-element.34), channel_id=1, source_target_pairs={{0,13},{1,14},{2,15},{3,0},{4,1},{5,2},{6,3},{7,4},{8,5},{9,6},{10... | collective-permute-start | bytes 393224 | tf_op jit(solution)/shard_map/ppermute | solution.py:27
  208.7 12.3 %collective-permute-start.17 = (bf16[1,64,32,1,32]{1,4,0,2,3:T(8,128)(2,1)S(1)}, bf16[1,64,32,1,32]{1,4,0,2,3:T(8,128)(2,1)S(1)}, u32[]{:S(2)}, u32[]{:S(2)}) collective-permute-start(bf16[1,64,32,1,32]{1,4,0,2,3:T(8,128)(2,1)S(1)} %get-tuple-element.33), channel_id=1, source_target_pairs={{0,14},{1,15},{2,0},{3,1},{4,2},{5,3},{6,4},{7,5},{8,6},{9,7},{10,... | collective-permute-start | bytes 393224 | tf_op jit(solution)/shard_map/ppermute | solution.py:27
  214.8 9.8 %collective-permute-start.18 = (bf16[1,64,32,1,32]{1,4,0,2,3:T(8,128)(2,1)S(1)}, bf16[1,64,32,1,32]{1,4,0,2,3:T(8,128)(2,1)S(1)}, u32[]{:S(2)}, u32[]{:S(2)}) collective-permute-start(bf16[1,64,32,1,32]{1,4,0,2,3:T(8,128)(2,1)S(1)} %get-tuple-element.32), channel_id=1, source_target_pairs={{0,15},{1,0},{2,1},{3,2},{4,3},{5,4},{6,5},{7,6},{8,7},{9,8},{10,9... | collective-permute-start | bytes 393224 | tf_op jit(solution)/shard_map/ppermute | solution.py:27
  239.5 14.8 %all-to-all-start.1 = ((bf16[37,32,2,256]{3,1,0,2:T(8,128)(2,1)}), bf16[37,32,2,256]{3,1,0,2:T(8,128)(2,1)}, u32[]{:S(2)}, u32[]{:S(2)}) async-start(bf16[37,32,2,256]{3,1,0,2:T(8,128)(2,1)} %copy.71), calls=%async_computation.1 | async-start | bytes 2424832 | tf_op jit(solution)/shard_map/all_to_all | solution.py:61
  243.9 186.3 %all-reduce.3.cloned.1.call-start = ((), (), s32[]{:S(2)}) async-start(), calls=%async_computation.2 | async-start | bytes 589824 | tf_op jit(solution)/shard_map/psum | solution.py:158
  260.5 19.8 %copy-start.2 = (bf16[64,64,256]{2,0,1:T(8,128)(2,1)}, bf16[64,64,256]{2,0,1:T(8,128)(2,1)S(1)}, u32[]{:S(2)}) copy-start(bf16[64,64,256]{2,0,1:T(8,128)(2,1)S(1)} %get-tuple-element.63) | copy-start | bytes 6291460
  271.3 8.3 %copy-start.10 = (bf16[64,64,256]{2,0,1:T(8,128)(2,1)S(1)}, bf16[64,64,256]{2,0,1:T(8,128)(2,1)}, u32[]{:S(2)}) copy-start(bf16[64,64,256]{2,0,1:T(8,128)(2,1)} %copy-done.8) | copy-start | bytes 6291460
  271.3 8.3 %copy-start.20 = (bf16[64,4,256]{2,0,1:T(8,128)(2,1)S(1)}, bf16[64,4,256]{2,0,1:T(8,128)(2,1)}, u32[]{:S(2)}) copy-start(bf16[64,4,256]{2,0,1:T(8,128)(2,1)} %copy-done.19) | copy-start | bytes 393220
  274.9 67.7 %collective-permute-start.20 = (bf16[64,4,256]{2,0,1:T(8,128)(2,1)S(1)}, bf16[64,4,256]{2,0,1:T(8,128)(2,1)S(1)}, u32[]{:S(2)}, u32[]{:S(2)}) collective-permute-start(bf16[64,4,256]{2,0,1:T(8,128)(2,1)S(1)} %get-tuple-element.53), channel_id=1, source_target_pairs={{2,0},{4,2},{6,4},{8,6},{10,8},{12,10},{14,12},{3,1},{5,3},{7,5},{... | collective-permute-start | bytes 393224 | tf_op jit(solution)/shard_map/ppermute | solution.py:42
  276.2 66.4 %collective-permute-start.19 = (bf16[64,4,256]{2,0,1:T(8,128)(2,1)S(1)}, bf16[64,4,256]{2,0,1:T(8,128)(2,1)S(1)}, u32[]{:S(2)}, u32[]{:S(2)}) collective-permute-start(bf16[64,4,256]{2,0,1:T(8,128)(2,1)S(1)} %get-tuple-element.54), channel_id=1, source_target_pairs={{0,2},{2,4},{4,6},{6,8},{8,10},{10,12},{12,14},{1,3},{3,5},{5,7},{... | collective-permute-start | bytes 393224 | tf_op jit(solution)/shard_map/ppermute | solution.py:40
  344.4 14.0 %copy-start.3 = (bf16[64,64,256]{2,0,1:T(8,128)(2,1)S(1)}, bf16[64,64,256]{2,0,1:T(8,128)(2,1)}, u32[]{:S(2)}) copy-start(bf16[64,64,256]{2,0,1:T(8,128)(2,1)} %copy-done.2) | copy-start | bytes 6291460
  349.4 16.1 %collective-permute-start.21 = (bf16[64,72,4]{1,0,2:T(8,128)(2,1)}, bf16[64,72,4]{1,0,2:T(8,128)(2,1)}, u32[]{:S(2)}, u32[]{:S(2)}) collective-permute-start(bf16[64,72,4]{1,0,2:T(8,128)(2,1)} %copy.73), channel_id=1, source_target_pairs={{1,0},{3,2},{5,4},{7,6},{9,8},{11,10},{13,12},{15,14},{17,16},{19,... | collective-permute-start | bytes 110600 | tf_op jit(solution)/shard_map/ppermute | solution.py:42
  352.7 15.6 %collective-permute-start.22 = (bf16[64,72,4]{1,0,2:T(8,128)(2,1)}, bf16[64,72,4]{1,0,2:T(8,128)(2,1)}, u32[]{:S(2)}, u32[]{:S(2)}) collective-permute-start(bf16[64,72,4]{1,0,2:T(8,128)(2,1)} %copy.77), channel_id=1, source_target_pairs={{0,1},{2,3},{4,5},{6,7},{8,9},{10,11},{12,13},{14,15},{16,17},{18,... | collective-permute-start | bytes 110600 | tf_op jit(solution)/shard_map/ppermute | solution.py:40
  392.8 39.1 %copy-start.1 = (bf16[37,64]{1,0:T(8,128)(2,1)S(1)}, bf16[37,64]{1,0:T(8,128)(2,1)}, u32[]{:S(2)}) copy-start(bf16[37,64]{1,0:T(8,128)(2,1)} %param.12) | copy-start | bytes 14212
  (23 other events, 78.8 us)
Sparse Core Ops, SparseCore 0:
  342.7 87.4 all-reduce.2
